TPU v7x, 128 devices: a whole 4x4x4 slice. The times are simulated.
128 devices in a mesh: gx: 8 (over z, x_hi), gy: 16 (over x_lo, y, core).
Axes of the slice: x: 4 (x_hi: 2, x_lo: 2; x = x_hi * 2 + x_lo), y: 4, z: 4, core: 2. Of those that a mesh axis runs over, the one named last changes fastest.
Arguments:
- source_planes: float32 [384, 384, 384], P(('gx', 'gy')), may hold values from -6 to 6
- weight_x: float32 [64, 384], replicated, may hold values from -0.3125 to 0.3125
- weight_y: float32 [96, 384], replicated, may hold values from -0.3125 to 0.3125
- weight_z: float32 [96, 384], replicated, may hold values from -0.3125 to 0.3125
- box_anchor: int32 [3], replicated, may hold values from 0 to 416, as said below
- velocity: float32 [3, 192, 512, 320], P(None, 'gx', 'gy'), may hold values from -6 to 6
- stress: float32 [6, 192, 512, 320], P(None, 'gx', 'gy'), may hold values from -6 to 6
- lame_lambda: float32 [192, 512, 320], P('gx', 'gy'), may hold values from 0.2 to 1
- lame_mu: float32 [192, 512, 320], P('gx', 'gy'), may hold values from 0.2 to 1
- buoyancy: float32 [192, 512, 320], P('gx', 'gy'), may hold values from 0.5 to 1.5
- attenuation: float32 [192, 512, 320], P('gx', 'gy'), may hold values from 0.05 to 3
Outputs:
- velocity_out: float32 [3, 192, 512, 320], P(None, 'gx', 'gy')
- stress_out: float32 [6, 192, 512, 320], P(None, 'gx', 'gy')
Inputs may be any that keep to these rules, and one draw needn't show every extreme that they name: The box of 64 x 96 x 96 cells that starts at box_anchor lies inside the thorax grid; along the dimension with the most room it ends at the grid's far side, along one of the other two it starts at cell 0.
All inputs are finite; a program needn't handle non-finite values.
Results may differ from a plain program's by a relative error of at most 0.00005.
Values sent between devices are 32-bit elements; how exact they have to be, the bound alone decides.
No kernel may reach another device: no remote copies, remote signals or barrier semaphores. Data moves between devices by JAX's collectives and lax.ppermute only.
A program may use at most 128 MiB of HBM per device.

v0:
```python
import jax
import jax.numpy as jnp
from jax import lax
from jax.sharding import PartitionSpec as P

STEPS = 2
time_step = 0.2
precise = lax.Precision.HIGHEST


def from_behind(value, axis, by):
    size = lax.axis_size(axis)
    pairs = [(i, i + by) for i in range(size) if 0 <= i + by < size]
    return lax.ppermute(value, axis, pairs)


def back_diff(values, dimension, beside):
    count = values.shape[dimension]
    return values - jnp.concatenate(
        [beside, lax.slice_in_dim(values, 0, count - 1, axis=dimension)], dimension
    )


def ahead_diff(values, dimension, beside):
    count = values.shape[dimension]
    return (
        jnp.concatenate([lax.slice_in_dim(values, 1, count, axis=dimension), beside], dimension)
        - values
    )


def one_hot(anchor, amount, box_start, extent):
    positions = anchor + lax.iota(jnp.int32, amount) - box_start
    return (positions[:, None] == lax.iota(jnp.int32, extent)[None, :]).astype(jnp.float32)


def shards(
    source_planes,
    weight_x,
    weight_y,
    weight_z,
    box_anchor,
    velocity,
    stress,
    lame_lambda,
    lame_mu,
    buoyancy,
    attenuation,
):
    rows_x = velocity.shape[1]
    rows_y = velocity.shape[2]
    cells_z = velocity.shape[3]
    box_x = weight_x.shape[0]
    box_y = weight_y.shape[0]
    box_z = weight_z.shape[0]
    reduced = jnp.einsum("abc,zc->abz", source_planes, weight_z, precision=precise)
    reduced = jnp.einsum("abz,yb->ayz", reduced, weight_y, precision=precise)
    own_planes = reduced.shape[0]
    own_start = lax.axis_index(("gx", "gy")) * own_planes
    weight_own = lax.dynamic_slice_in_dim(weight_x, own_start, own_planes, 1)
    partial_box = jnp.einsum("xa,ayz->xyz", weight_own, reduced, precision=precise)
    whole_box = lax.psum(partial_box, ("gx", "gy"))
    place_x = one_hot(lax.axis_index("gx") * rows_x, rows_x, box_anchor[0], box_x)
    box_rows = jnp.einsum("Xx,xyz->Xyz", place_x, whole_box, precision=precise)
    place_y = one_hot(lax.axis_index("gy") * rows_y, rows_y, box_anchor[1], box_y)
    place_z = one_hot(0, cells_z, box_anchor[2], box_z)
    pressure = jnp.einsum("xyz,Yy->xYz", box_rows, place_y, precision=precise)
    pressure = jnp.einsum("xYz,Zz->xYZ", pressure, place_z, precision=precise)
    decay = jnp.exp(-time_step * attenuation)
    zero_z = jnp.zeros((rows_x, rows_y, 1), jnp.float32)
    speed_x, speed_y, speed_z = (velocity[0], velocity[1], velocity[2])
    stress_xx, stress_yy, stress_zz = (stress[0], stress[1], stress[2])
    stress_xy, stress_xz, stress_yz = (stress[3], stress[4], stress[5])
    for stepping in range(STEPS):
        lower_x = from_behind(jnp.stack([stress_xx[-1], stress_xy[-1], stress_xz[-1]]), "gx", 1)
        lower_y = from_behind(
            jnp.stack([stress_xy[:, -1], stress_yy[:, -1], stress_yz[:, -1]]), "gy", 1
        )
        speed_x = speed_x + time_step * buoyancy * (
            back_diff(stress_xx, 0, lower_x[0][None])
            + back_diff(stress_xy, 1, lower_y[0][:, None])
            + back_diff(stress_xz, 2, zero_z)
        )
        speed_y = speed_y + time_step * buoyancy * (
            back_diff(stress_xy, 0, lower_x[1][None])
            + back_diff(stress_yy, 1, lower_y[1][:, None])
            + back_diff(stress_yz, 2, zero_z)
        )
        speed_z = speed_z + time_step * buoyancy * (
            back_diff(stress_xz, 0, lower_x[2][None])
            + back_diff(stress_yz, 1, lower_y[2][:, None])
            + back_diff(stress_zz, 2, zero_z)
        )
        upper_x = from_behind(jnp.stack([speed_x[0], speed_y[0], speed_z[0]]), "gx", -1)
        upper_y = from_behind(jnp.stack([speed_x[:, 0], speed_y[:, 0], speed_z[:, 0]]), "gy", -1)
        strain_xx = ahead_diff(speed_x, 0, upper_x[0][None])
        strain_yy = ahead_diff(speed_y, 1, upper_y[1][:, None])
        strain_zz = ahead_diff(speed_z, 2, zero_z)
        trace = strain_xx + strain_yy + strain_zz
        shear_xy = ahead_diff(speed_x, 1, upper_y[0][:, None]) + ahead_diff(
            speed_y, 0, upper_x[1][None]
        )
        shear_xz = ahead_diff(speed_x, 2, zero_z) + ahead_diff(speed_z, 0, upper_x[2][None])
        shear_yz = ahead_diff(speed_y, 2, zero_z) + ahead_diff(speed_z, 1, upper_y[2][:, None])
        stress_xx = decay * (
            stress_xx
            + time_step * (lame_lambda * trace + 2.0 * lame_mu * strain_xx)
            - time_step * pressure
        )
        stress_yy = decay * (
            stress_yy
            + time_step * (lame_lambda * trace + 2.0 * lame_mu * strain_yy)
            - time_step * pressure
        )
        stress_zz = decay * (
            stress_zz
            + time_step * (lame_lambda * trace + 2.0 * lame_mu * strain_zz)
            - time_step * pressure
        )
        stress_xy = decay * (stress_xy + time_step * lame_mu * shear_xy)
        stress_xz = decay * (stress_xz + time_step * lame_mu * shear_xz)
        stress_yz = decay * (stress_yz + time_step * lame_mu * shear_yz)
    velocity_out = jnp.stack([speed_x, speed_y, speed_z])
    stress_out = jnp.stack([stress_xx, stress_yy, stress_zz, stress_xy, stress_xz, stress_yz])
    return (velocity_out, stress_out)


def solution(mesh):
    in_specs = (
        P(("gx", "gy"), None, None),
        P(),
        P(),
        P(),
        P(),
        P(None, "gx", "gy", None),
        P(None, "gx", "gy", None),
        P("gx", "gy", None),
        P("gx", "gy", None),
        P("gx", "gy", None),
        P("gx", "gy", None),
    )
    out_specs = (P(None, "gx", "gy", None), P(None, "gx", "gy", None))
    return jax.shard_map(shards, mesh=mesh, in_specs=in_specs, out_specs=out_specs, check_vma=False)
```

profile of v0, /device:TPU:6, one launch (start us, length us, event | category | flops | bytes accessed | tf_op | source)
XLA Modules:
  0.0 261.1 jit_solution(14584826044277785940)
XLA Ops:
  7.2 4.8 %slice_bitcast_fusion.1 = (f32[24,32,320]{2,1,0:T(8,128)}, f32[24,32,320]{2,1,0:T(8,128)S(1)}, f32[24,32,320]{2,1,0:T(8,128)S(1)}, f32[24,32,320]{2,1,0:T(8,128)S(1)}, f32[24,32,320]{2,1,0:T(8,128)}) fusion(f32[6,24,32,320]{3,2,1,0:T(8,128)} %param.17), kind=kLoop, calls=%fused_computation.98 | loop fusion | bytes 9830400 | tf_op jit(solution)/shard_map/squeeze | solution.py:73
  12.1 1.0 copy-done.20
  13.1 0.3 copy-done.22
  13.6 1.9 collective-permute-start.1
  15.5 0.9 slice_bitcast_fusion.10
  16.4 4.7 %collective-permute-start = (f32[3,32,320]{2,1,0:T(8,128)S(1)}, f32[3,32,320]{2,1,0:T(8,128)S(1)}, u32[]{:S(2)}, u32[]{:S(2)}) collective-permute-start(f32[3,32,320]{2,1,0:T(8,128)S(1)} %pad_maximum_fusion.1), channel_id=1, source_target_pairs={{0,16},{16,32},{32,48},{48,64},{64,80},{80,96},{96,112},{1,17},{17... | collective-permute-start | bytes 368648 | tf_op jit(solution)/shard_map/ppermute | solution.py:14
  21.1 1.6 fusion.60
  22.7 1.1 convolution_bitcast_fusion.1
  23.9 3.5 %fusion.65 = f32[64,96,96]{2,0,1:T(8,128)S(1)} fusion(f32[3,96,96]{2,0,1:T(4,128)S(1)} %copy.13, f32[64,384]{1,0:T(8,128)} %param.12, s32[]{:T(128)S(6)} %select_n.3), kind=kOutput, calls=%fused_computation.147 | convolution fusion | flops 21233664 | bytes 2502660 | tf_op jit(solution)/shard_map/xa,ayz->xyz/dot_general | solution.py:61
  27.5 3.5 %copy.14 = f32[64,96,96]{2,1,0:T(8,128)} copy(f32[64,96,96]{2,0,1:T(8,128)S(1)} %fusion.65) | data formatting | bytes 4718592 | tf_op jit(solution)/shard_map/xa,ayz->xyz/dot_general | solution.py:61
  31.0 3.9 %slice_bitcast_fusion.7 = (f32[23,32,320]{2,1,0:T(8,128)}, f32[23,32,320]{2,1,0:T(8,128)}, f32[23,32,320]{2,1,0:T(8,128)}) fusion(f32[6,24,32,320]{3,2,1,0:T(8,128)} %param.17), kind=kLoop, calls=%fused_computation.105 | loop fusion | bytes 5652480 | tf_op jit(solution)/shard_map/slice | solution.py:20
  34.9 0.7 fusion.79
  35.6 0.7 iota_subtract_fusion
  36.3 0.7 add_subtract_fusion
  37.0 0.6 add_subtract_fusion.1
  37.7 1.2 slice_bitcast_fusion.31
  38.9 6.4 %fusion.5 = (f32[24,32,320]{2,1,0:T(8,128)S(1)}, f32[24,32,320]{2,1,0:T(8,128)S(1)}) fusion(f32[23,32,320]{2,1,0:T(8,128)} %get-tuple-element.17, f32[1,32,320]{2,1,0:T(8,128)S(1)} %get-tuple-element.46, f32[24,31,320]{2,1,0:T(8,128)} %bitcast.189, f32[24,1,320]{2,1,0:T(1,128)S(1)} %get-tuple-element.43, f32[24,32,319]{2,1,0:T(8,128)} %bitcast.190, ...), kind=kLoop, calls=%fused_computation.9 | loop fusion | flops 4669440 | bytes 15722496 | tf_op jit(solution)/shard_map/add | solution.py:79
  45.5 0.9 slice-done.1
  46.3 1.0 copy-done.21
  47.3 0.5 copy-done.25
  47.8 2.4 fusion.9
  50.3 1.2 slice.421
  51.4 1.4 slice.439
  52.8 1.2 slice.455
  54.1 1.2 slice.434
  55.3 1.4 slice.454
  56.7 1.2 slice.441
  57.8 0.4 slice.446
  58.4 5.1 %collective-permute-start.3 = (f32[3,24,320]{2,0,1:T(4,128)S(1)}, f32[3,24,320]{2,0,1:T(4,128)S(1)}, u32[]{:S(2)}, u32[]{:S(2)}) collective-permute-start(f32[3,24,320]{2,0,1:T(4,128)S(1)} %pad_maximum_fusion.4), channel_id=1, source_target_pairs={{1,0},{2,1},{3,2},{4,3},{5,4},{6,5},{7,6},{8,7},{9,8},{10,9},{11,1... | collective-permute-start | bytes 276488 | tf_op jit(solution)/shard_map/ppermute | solution.py:14
  63.5 4.1 %collective-permute-start.2 = (f32[3,32,320]{2,1,0:T(8,128)S(1)}, f32[3,32,320]{2,1,0:T(8,128)S(1)}, u32[]{:S(2)}, u32[]{:S(2)}) collective-permute-start(f32[3,32,320]{2,1,0:T(8,128)S(1)} %pad_maximum_fusion.3), channel_id=1, source_target_pairs={{16,0},{32,16},{48,32},{64,48},{80,64},{96,80},{112,96},{17,1},{33... | collective-permute-start | bytes 368648 | tf_op jit(solution)/shard_map/ppermute | solution.py:14
  67.8 5.4 %collective-permute-done.2 = f32[3,32,320]{2,1,0:T(8,128)S(1)} collective-permute-done((f32[3,32,320]{2,1,0:T(8,128)S(1)}, f32[3,32,320]{2,1,0:T(8,128)S(1)}, u32[]{:S(2)}, u32[]{:S(2)}) %collective-permute-start.2) | collective-permute-done | bytes 122912 | tf_op jit(solution)/shard_map/ppermute | solution.py:14
  73.2 0.9 fusion.21
  74.2 1.0 copy-done.11
  75.2 1.1 slice.467
  76.2 109.6 %all-reduce.14.cloned.1.call-done = f32[64,96,96]{2,1,0:T(8,128)} async-done(((f32[64,96,96]{2,1,0:T(8,128)}), f32[64,96,96]{2,1,0:T(8,128)}) %all-reduce.14.cloned.1.call-update) | async-done | bytes 2359312 | tf_op jit(solution)/shard_map/psum | solution.py:62
  185.9 4.9 %fusion = f32[24,96,96]{2,0,1:T(8,128)S(1)} fusion(f32[64,96,96]{2,1,0:T(8,128)} %all-reduce.14.cloned.1.call-done, s32[24]{0:T(128)S(1)} %add_subtract_fusion), kind=kOutput, calls=%fused_computation.1 | convolution fusion | flops 169870848 | bytes 3244128 | tf_op jit(solution)/shard_map/Xx,xyz->Xyz/dot_general | solution.py:64
  190.8 0.6 convolution_bitcast_fusion
  191.5 0.6 copy-done.6
  192.0 5.2 %subtract_multiply_fusion = (f32[24,32,320]{2,1,0:T(8,128)}, f32[24,32,320]{2,1,0:T(8,128)S(1)}, f32[24,32,320]{2,1,0:T(8,128)S(1)}, f32[24,32,320]{2,1,0:T(8,128)S(1)}) fusion(f32[24,32,320]{2,1,0:T(8,128)S(1)} %copy-done.2, f32[24,32,320]{2,1,0:T(8,128)S(1)} %copy-done.8, f32[24,32,319]{2,1,0:T(8,128)} %slice.439, f32[6,24,32,320]{3,2,1,0:T(8,128)} %param.17, ...), kind=kOutput, calls=%fused_computation.92 | convolution fusion | flops 289290240 | bytes 17001728 | tf_op jit(solution)/shard_map/xYz,Zz->xYZ/dot_general | solution.py:68
  197.2 0.5 copy-done.24
  197.7 2.2 subtract_multiply_fusion.1
  200.0 0.9 copy-done.16
  200.9 1.1 slice.451
  202.2 1.9 collective-permute-start.5
  204.1 3.5 %collective-permute-start.4 = (f32[3,32,320]{2,1,0:T(8,128)S(1)}, f32[3,32,320]{2,1,0:T(8,128)S(1)}, u32[]{:S(2)}, u32[]{:S(2)}) collective-permute-start(f32[3,32,320]{2,1,0:T(8,128)S(1)} %pad_maximum_fusion.5), channel_id=1, source_target_pairs={{0,16},{16,32},{32,48},{48,64},{64,80},{80,96},{96,112},{1,17},{17... | collective-permute-start | bytes 368648 | tf_op jit(solution)/shard_map/ppermute | solution.py:14
  207.6 3.1 %collective-permute-done.5 = f32[3,24,320]{2,0,1:T(4,128)S(1)} collective-permute-done((f32[3,24,320]{2,0,1:T(4,128)S(1)}, f32[3,24,320]{2,0,1:T(4,128)S(1)}, u32[]{:S(2)}, u32[]{:S(2)}) %collective-permute-start.5) | collective-permute-done | bytes 92192 | tf_op jit(solution)/shard_map/ppermute | solution.py:14
  210.8 3.1 %collective-permute-done.4 = f32[3,32,320]{2,1,0:T(8,128)S(1)} collective-permute-done((f32[3,32,320]{2,1,0:T(8,128)S(1)}, f32[3,32,320]{2,1,0:T(8,128)S(1)}, u32[]{:S(2)}, u32[]{:S(2)}) %collective-permute-start.4) | collective-permute-done | bytes 122912 | tf_op jit(solution)/shard_map/ppermute | solution.py:14
  213.9 1.1 fusion.33
  215.2 5.1 %fusion.25 = (f32[24,32,320]{2,1,0:T(8,128)S(1)}, f32[24,32,320]{2,1,0:T(8,128)S(1)}) fusion(f32[24,32,320]{2,1,0:T(8,128)S(1)} %copy-done.6, f32[24,32,320]{2,1,0:T(8,128)} %copy-done.16, f32[23,32,320]{2,1,0:T(8,128)} %slice.451, f32[1,32,320]{2,1,0:T(8,128)S(1)} %get-tuple-element.34, f32[24,32,320]{2,1,0:T(8,128)S(1)} %get-tuple-element.8, ...), kind=kLoop, calls=%fused_computation.40 | loop fusion | flops 4669440 | bytes 15722496 | tf_op jit(solution)/shard_map/add | solution.py:79
  220.5 0.4 slice.481
  220.9 1.1 slice.471
  221.9 1.1 slice.484
  223.2 0.4 slice.486
  223.7 0.4 slice.489
  224.3 4.6 %collective-permute-start.7 = (f32[3,24,320]{2,0,1:T(4,128)S(1)}, f32[3,24,320]{2,0,1:T(4,128)S(1)}, u32[]{:S(2)}, u32[]{:S(2)}) collective-permute-start(f32[3,24,320]{2,0,1:T(4,128)S(1)} %pad_maximum_fusion.8), channel_id=1, source_target_pairs={{1,0},{2,1},{3,2},{4,3},{5,4},{6,5},{7,6},{8,7},{9,8},{10,9},{11,1... | collective-permute-start | bytes 276488 | tf_op jit(solution)/shard_map/ppermute | solution.py:14
  228.9 2.1 pad_maximum_fusion
  231.0 2.6 collective-permute-start.6
  233.7 6.8 %collective-permute-done.6 = f32[3,32,320]{2,1,0:T(8,128)S(1)} collective-permute-done((f32[3,32,320]{2,1,0:T(8,128)S(1)}, f32[3,32,320]{2,1,0:T(8,128)S(1)}, u32[]{:S(2)}, u32[]{:S(2)}) %collective-permute-start.6) | collective-permute-done | bytes 122912 | tf_op jit(solution)/shard_map/ppermute | solution.py:14
  240.5 3.8 %bitcast_dynamic-update-slice_fusion.2 = (f32[6,24,32,320]{3,2,1,0:T(8,128)}, f32[24,32,320]{2,1,0:T(8,128)S(1)}) fusion(f32[24,32,320]{2,1,0:T(8,128)S(1)} %get-tuple-element.52, f32[24,32,320]{2,1,0:T(8,128)S(1)} %copy-done.17, f32[24,32,320]{2,1,0:T(8,128)S(1)} %copy-done.2, f32[24,32,320]{2,1,0:T(8,128)S(1)} %get-tuple-element.23, ...), kind=kLoop, calls=%fused_computation.85 | loop fusion | flops 3932159 | bytes 12973056
  244.3 2.0 bitcast_dynamic-update-slice_fusion.1
  246.3 2.0 bitcast_dynamic-update-slice_fusion
  248.3 2.0 fusion.43
  250.3 2.0 fusion.49
  252.3 2.0 fusion.55
  (112 shorter events, 2.3 us)
Async XLA Ops:
  7.2 13.9 %copy-start = (f32[3,384,384]{2,1,0:T(8,128)S(1)}, f32[3,384,384]{2,1,0:T(8,128)}, u32[]{:S(2)}) copy-start(f32[3,384,384]{2,1,0:T(8,128)} %param.11) | copy-start | bytes 5308420
  7.2 178.7 %all-reduce.14.cloned.1.call-start = ((), (), s32[]{:S(2)}) async-start(), calls=%async_computation | async-start | bytes 6291456 | tf_op jit(solution)/shard_map/psum | solution.py:62
  12.0 1.0 copy-start.20
  12.0 1.4 copy-start.22
  12.0 9.0 %copy-start.27 = (f32[96,384]{1,0:T(8,128)S(1)}, f32[96,384]{1,0:T(8,128)}, u32[]{:S(2)}) copy-start(f32[96,384]{1,0:T(8,128)} %param.14) | copy-start | bytes 442372
  13.6 24.1 %collective-permute-start.1 = (f32[3,24,320]{2,0,1:T(4,128)S(1)}, f32[3,24,320]{2,0,1:T(4,128)}, u32[]{:S(2)}, u32[]{:S(2)}) collective-permute-start(f32[3,24,320]{2,0,1:T(4,128)S(1)} %pad_maximum_fusion.2), channel_id=1, source_target_pairs={{0,1},{1,2},{2,3},{3,4},{4,5},{5,6},{6,7},{7,8},{8,9},{9,10},{10,1... | collective-permute-start | bytes 276488 | tf_op jit(solution)/shard_map/ppermute | solution.py:14
  16.4 22.5 %collective-permute-start = (f32[3,32,320]{2,1,0:T(8,128)S(1)}, f32[3,32,320]{2,1,0:T(8,128)S(1)}, u32[]{:S(2)}, u32[]{:S(2)}) collective-permute-start(f32[3,32,320]{2,1,0:T(8,128)S(1)} %pad_maximum_fusion.1), channel_id=1, source_target_pairs={{0,16},{16,32},{32,48},{48,64},{64,80},{80,96},{96,112},{1,17},{17... | collective-permute-start | bytes 368648 | tf_op jit(solution)/shard_map/ppermute | solution.py:14
  21.1 1.6 copy-start.28
  31.0 4.0 %copy-start.29 = (s32[3]{0:T(128)S(1)}, s32[3]{0:T(128)}, u32[]{:S(2)}) copy-start(s32[3]{0:T(128)} %param.15) | copy-start | bytes 40
  31.0 7.9 %copy-start.13 = (f32[24,32,320]{2,1,0:T(8,128)S(1)}, f32[24,32,320]{2,1,0:T(8,128)}, u32[]{:S(2)}) copy-start(f32[24,32,320]{2,1,0:T(8,128)} %param.20) | copy-start | bytes 2949124
  38.9 6.6 %slice-start = ((s8[7077888]{0:T(1024)(128)(4,1)}), s8[4194304]{0:T(1024)(128)(4,1)S(1)}, s32[]{:S(2)}) async-start(s8[7077888]{0:T(1024)(128)(4,1)} %bitcast.175), calls=%async_computation.1 | async-start | bytes 8388608
  38.9 7.5 %slice-start.1 = ((s8[7077888]{0:T(1024)(128)(4,1)}), s8[2883584]{0:T(1024)(128)(4,1)S(1)}, s32[]{:S(2)}) async-start(s8[7077888]{0:T(1024)(128)(4,1)} %bitcast.175), calls=%async_computation.2 | async-start | bytes 5767168
  38.9 8.4 %copy-start.21 = (f32[24,32,320]{2,1,0:T(8,128)S(1)}, f32[24,32,320]{2,1,0:T(8,128)}, u32[]{:S(2)}) copy-start(f32[24,32,320]{2,1,0:T(8,128)} %copy-done.20) | copy-start | bytes 2949124
  38.9 8.9 %copy-start.25 = (f32[23,32,320]{2,1,0:T(8,128)S(1)}, f32[23,32,320]{2,1,0:T(8,128)}, u32[]{:S(2)}) copy-start(f32[23,32,320]{2,1,0:T(8,128)} %get-tuple-element.18) | copy-start | bytes 2826244
  45.4 27.8 %copy-start.5 = (f32[24,32,320]{2,1,0:T(8,128)}, f32[24,32,320]{2,1,0:T(8,128)S(1)}, u32[]{:S(2)}) copy-start(f32[24,32,320]{2,1,0:T(8,128)S(1)} %get-tuple-element.10) | copy-start | bytes 2949124
  45.4 27.8 %copy-start.7 = (f32[24,32,320]{2,1,0:T(8,128)}, f32[24,32,320]{2,1,0:T(8,128)S(1)}, u32[]{:S(2)}) copy-start(f32[24,32,320]{2,1,0:T(8,128)S(1)} %get-tuple-element.11) | copy-start | bytes 2949124
  50.2 7.6 %copy-start.9 = (f32[24,32,320]{2,1,0:T(8,128)}, f32[24,32,320]{2,1,0:T(8,128)S(1)}, u32[]{:S(2)}) copy-start(f32[24,32,320]{2,1,0:T(8,128)S(1)} %fusion.9) | copy-start | bytes 2949124
  58.2 5.3 %slice-start.4 = ((f32[24,32,320]{2,1,0:T(8,128)}), f32[1,32,320]{2,1,0:T(8,128)S(1)}, s32[]{:S(2)}) async-start(f32[24,32,320]{2,1,0:T(8,128)} %copy-done.9), calls=%async_computation.5 | async-start | bytes 98304 | tf_op jit(solution)/shard_map/slice | solution.py:94
  58.2 15.0 %copy-start.2 = (f32[24,32,320]{2,1,0:T(8,128)S(1)}, f32[24,32,320]{2,1,0:T(8,128)}, u32[]{:S(2)}) copy-start(f32[24,32,320]{2,1,0:T(8,128)} %param.19) | copy-start | bytes 2949124
  58.2 15.0 %copy-start.3 = (f32[24,32,320]{2,1,0:T(8,128)S(1)}, f32[24,32,320]{2,1,0:T(8,128)}, u32[]{:S(2)}) copy-start(f32[24,32,320]{2,1,0:T(8,128)} %param.21) | copy-start | bytes 2949124
  58.4 9.3 %collective-permute-start.3 = (f32[3,24,320]{2,0,1:T(4,128)S(1)}, f32[3,24,320]{2,0,1:T(4,128)S(1)}, u32[]{:S(2)}, u32[]{:S(2)}) collective-permute-start(f32[3,24,320]{2,0,1:T(4,128)S(1)} %pad_maximum_fusion.4), channel_id=1, source_target_pairs={{1,0},{2,1},{3,2},{4,3},{5,4},{6,5},{7,6},{8,7},{9,8},{10,9},{11,1... | collective-permute-start | bytes 276488 | tf_op jit(solution)/shard_map/ppermute | solution.py:14
  63.5 9.6 %collective-permute-start.2 = (f32[3,32,320]{2,1,0:T(8,128)S(1)}, f32[3,32,320]{2,1,0:T(8,128)S(1)}, u32[]{:S(2)}, u32[]{:S(2)}) collective-permute-start(f32[3,32,320]{2,1,0:T(8,128)S(1)} %pad_maximum_fusion.3), channel_id=1, source_target_pairs={{16,0},{32,16},{48,32},{64,48},{80,64},{96,80},{112,96},{17,1},{33... | collective-permute-start | bytes 368648 | tf_op jit(solution)/shard_map/ppermute | solution.py:14
  74.2 1.0 copy-start.11
  185.9 5.6 %copy-start.8 = (f32[24,32,320]{2,1,0:T(8,128)S(1)}, f32[24,32,320]{2,1,0:T(8,128)}, u32[]{:S(2)}) copy-start(f32[24,32,320]{2,1,0:T(8,128)} %copy-done.7) | copy-start | bytes 2949124
  185.9 5.6 %copy-start.10 = (f32[24,32,320]{2,1,0:T(8,128)S(1)}, f32[24,32,320]{2,1,0:T(8,128)}, u32[]{:S(2)}) copy-start(f32[24,32,320]{2,1,0:T(8,128)} %copy-done.9) | copy-start | bytes 2949124
  185.9 5.6 %copy-start.18 = (f32[24,31,320]{2,1,0:T(8,128)S(1)}, f32[24,31,320]{2,1,0:T(8,128)}, u32[]{:S(2)}) copy-start(f32[24,31,320]{2,1,0:T(8,128)} %slice.434) | copy-start | bytes 2856964
  185.9 5.6 %copy-start.19 = (f32[23,32,320]{2,1,0:T(8,128)S(1)}, f32[23,32,320]{2,1,0:T(8,128)}, u32[]{:S(2)}) copy-start(f32[23,32,320]{2,1,0:T(8,128)} %slice.421) | copy-start | bytes 2826244
  190.8 1.3 copy-start.6
  191.4 5.8 %slice-start.2 = ((s8[7077888]{0:T(1024)(128)(4,1)}), s8[4194304]{0:T(1024)(128)(4,1)S(1)}, s32[]{:S(2)}) async-start(s8[7077888]{0:T(1024)(128)(4,1)} %bitcast.177), calls=%async_computation.3 | async-start | bytes 8388608
  192.0 5.2 %slice-start.3 = ((s8[7077888]{0:T(1024)(128)(4,1)}), s8[2883584]{0:T(1024)(128)(4,1)S(1)}, s32[]{:S(2)}) async-start(s8[7077888]{0:T(1024)(128)(4,1)} %bitcast.177), calls=%async_computation.4 | async-start | bytes 5767168
  192.0 5.2 %slice-start.5 = ((f32[24,32,320]{2,1,0:T(8,128)}), f32[23,32,320]{2,1,0:T(8,128)S(1)}, s32[]{:S(2)}) async-start(f32[24,32,320]{2,1,0:T(8,128)} %copy-done.9), calls=%async_computation.6 | async-start | bytes 2260992 | tf_op jit(solution)/shard_map/slice | solution.py:27
  192.0 5.6 %copy-start.24 = (f32[24,31,320]{2,1,0:T(8,128)S(1)}, f32[24,31,320]{2,1,0:T(8,128)}, u32[]{:S(2)}) copy-start(f32[24,31,320]{2,1,0:T(8,128)} %slice.441) | copy-start | bytes 2856964
  199.9 1.0 copy-start.16
  200.9 13.0 %copy-start.14 = (f32[24,32,320]{2,1,0:T(8,128)S(1)}, f32[24,32,320]{2,1,0:T(8,128)}, u32[]{:S(2)}) copy-start(f32[24,32,320]{2,1,0:T(8,128)} %param.20) | copy-start | bytes 2949124
  202.2 8.6 %collective-permute-start.5 = (f32[3,24,320]{2,0,1:T(4,128)S(1)}, f32[3,24,320]{2,0,1:T(4,128)S(1)}, u32[]{:S(2)}, u32[]{:S(2)}) collective-permute-start(f32[3,24,320]{2,0,1:T(4,128)S(1)} %pad_maximum_fusion.6), channel_id=1, source_target_pairs={{0,1},{1,2},{2,3},{3,4},{4,5},{5,6},{6,7},{7,8},{8,9},{9,10},{10,1... | collective-permute-start | bytes 276488 | tf_op jit(solution)/shard_map/ppermute | solution.py:14
  204.1 9.8 %collective-permute-start.4 = (f32[3,32,320]{2,1,0:T(8,128)S(1)}, f32[3,32,320]{2,1,0:T(8,128)S(1)}, u32[]{:S(2)}, u32[]{:S(2)}) collective-permute-start(f32[3,32,320]{2,1,0:T(8,128)S(1)} %pad_maximum_fusion.5), channel_id=1, source_target_pairs={{0,16},{16,32},{32,48},{48,64},{64,80},{80,96},{96,112},{1,17},{17... | collective-permute-start | bytes 368648 | tf_op jit(solution)/shard_map/ppermute | solution.py:14
  213.9 1.3 copy-start.12
  224.3 9.3 %collective-permute-start.7 = (f32[3,24,320]{2,0,1:T(4,128)S(1)}, f32[3,24,320]{2,0,1:T(4,128)S(1)}, u32[]{:S(2)}, u32[]{:S(2)}) collective-permute-start(f32[3,24,320]{2,0,1:T(4,128)S(1)} %pad_maximum_fusion.8), channel_id=1, source_target_pairs={{1,0},{2,1},{3,2},{4,3},{5,4},{6,5},{7,6},{8,7},{9,8},{10,9},{11,1... | collective-permute-start | bytes 276488 | tf_op jit(solution)/shard_map/ppermute | solution.py:14
  228.9 11.6 %copy-start.17 = (f32[24,32,320]{2,1,0:T(8,128)S(1)}, f32[24,32,320]{2,1,0:T(8,128)}, u32[]{:S(2)}) copy-start(f32[24,32,320]{2,1,0:T(8,128)} %copy-done.16) | copy-start | bytes 2949124
  228.9 11.6 %copy-start.23 = (f32[24,32,320]{2,1,0:T(8,128)S(1)}, f32[24,32,320]{2,1,0:T(8,128)}, u32[]{:S(2)}) copy-start(f32[24,32,320]{2,1,0:T(8,128)} %param.18) | copy-start | bytes 2949124
  231.0 9.4 %collective-permute-start.6 = (f32[3,32,320]{2,1,0:T(8,128)S(1)}, f32[3,32,320]{2,1,0:T(8,128)S(1)}, u32[]{:S(2)}, u32[]{:S(2)}) collective-permute-start(f32[3,32,320]{2,1,0:T(8,128)S(1)} %pad_maximum_fusion.7), channel_id=1, source_target_pairs={{16,0},{32,16},{48,32},{64,48},{80,64},{96,80},{112,96},{17,1},{33... | collective-permute-start | bytes 368648 | tf_op jit(solution)/shard_map/ppermute | solution.py:14
  244.3 2.0 copy-start.15
  246.3 2.0 copy-start.26
  250.3 2.0 copy-start.4
  252.2 2.0 copy-start.1
Sparse Core Ops, SparseCore 0:
  31.1 154.7 all-reduce.13
where the time goes:
time: 262 us; the launch traced here: 261 us
  waiting for transfers between devices  128 us (49%)
  local copies, waits for them, and re-layouts  36.5 us (14%)
  other arithmetic  36.4 us (14%)
  starting transfers between devices  28.4 us (11%)
  matrix products  16.9 us (6%)
  between operations  14.9 us (6%)
    psum x1, waiting for transfers between devices, shards(): whole_box = lax.psum(partial_box, ('gx', 'gy'))  110 us
    ppermute x8, starting transfers between devices, from_behind(): return lax.ppermute(value, axis, pairs)  28.4 us
    ppermute x8, waiting for transfers between devices, from_behind(): return lax.ppermute(value, axis, pairs)  18.4 us
    unnamed x7, other arithmetic  11.8 us
    slice x19, local copies, waits for them, and re-layouts, ahead_diff(): lax.slice_in_dim(values, 1, count, axis=dimension)  11.8 us
    add x2, other arithmetic, shards(): speed_x + time_step * buoyancy * (back_diff(stress_xx, 0, lower_x[0][None...  11.6 us
    unnamed x68, local copies, waits for them, and re-layouts  6.77 us
    slice x4, local copies, waits for them, and re-layouts, back_diff(): lax.slice_in_dim(values, 0, count - 1, axis=dimension)  6.17 us
  transfers between devices with their start and end apart: 9, of which 5 were waited for; matrix products, arithmetic and copies ran while one was open for 15% of the time, Pallas kernels for 0%

commit v1 on v0

--- a/solution.py
+++ b/solution.py
@@ -59,7 +59,7 @@
     own_start = lax.axis_index(("gx", "gy")) * own_planes
     weight_own = lax.dynamic_slice_in_dim(weight_x, own_start, own_planes, 1)
     partial_box = jnp.einsum("xa,ayz->xyz", weight_own, reduced, precision=precise)
-    whole_box = lax.psum(partial_box, ("gx", "gy"))
+    whole_box = lax.psum(lax.psum(partial_box, "gy"), "gx")
     place_x = one_hot(lax.axis_index("gx") * rows_x, rows_x, box_anchor[0], box_x)
     box_rows = jnp.einsum("Xx,xyz->Xyz", place_x, whole_box, precision=precise)
     place_y = one_hot(lax.axis_index("gy") * rows_y, rows_y, box_anchor[1], box_y)

time: 262 us -> 376 us (1.44)
  waiting for transfers between devices: 128 us -> 239 us
    psum x1 -> x2, waiting for transfers between devices: 110 us -> 215 us  [shards(): whole_box = lax.psum(lax.psum(partial_box, 'gy'), 'gx')]
    ppermute x8, waiting for transfers between devices: 18.4 us -> 24 us  [from_behind(): return lax.ppermute(value, axis, pairs)]
    unnamed x68 -> x62, local copies, waits for them, and re-layouts: 6.77 us -> 7.75 us
    unnamed x7 -> x6, other arithmetic: 11.8 us -> 11.8 us
  transfers between devices with their start and end apart: 9 -> 10, of which waited for: 5 -> 7; matrix products, arithmetic and copies ran while one was open for 15% -> 10% of each run, Pallas kernels for 0% -> 0%
where the time goes in v1:
time: 376 us; the launch traced here: 374 us
  waiting for transfers between devices  239 us (64%)
  other arithmetic  38.3 us (10%)
  local copies, waits for them, and re-layouts  36.4 us (10%)
  starting transfers between devices  27.7 us (7%)
  matrix products  17.8 us (5%)
  between operations  14.8 us (4%)
    psum x2, waiting for transfers between devices, shards(): whole_box = lax.psum(lax.psum(partial_box, 'gy'), 'gx')  215 us
    ppermute x8, starting transfers between devices, from_behind(): return lax.ppermute(value, axis, pairs)  27.7 us
    ppermute x8, waiting for transfers between devices, from_behind(): return lax.ppermute(value, axis, pairs)  24 us
    slice x19, local copies, waits for them, and re-layouts, ahead_diff(): lax.slice_in_dim(values, 1, count, axis=dimension)  11.9 us
    unnamed x6, other arithmetic  11.8 us
    add x2, other arithmetic, shards(): speed_x + time_step * buoyancy * (back_diff(stress_xx, 0, lower_x[0][None...  11.1 us
    unnamed x62, local copies, waits for them, and re-layouts  7.75 us
  transfers between devices with their start and end apart: 10, of which 7 were waited for; matrix products, arithmetic and copies ran while one was open for 10% of the time, Pallas kernels for 0%

profile of v1, /device:TPU:6, one launch (start us, length us, event | category | flops | bytes accessed | tf_op | source)
XLA Modules:
  0.0 374.3 jit_solution(16402714472254907254)
XLA Ops:
  7.2 1.4 copy-done
  8.7 2.5 fusion.60
  11.2 1.1 convolution_bitcast_fusion.1
  12.5 3.5 fusion.65
  16.0 3.5 copy.14
  19.5 4.8 %slice_bitcast_fusion.1 = (f32[24,32,320]{2,1,0:T(8,128)}, f32[24,32,320]{2,1,0:T(8,128)S(1)}, f32[24,32,320]{2,1,0:T(8,128)S(1)}, f32[24,32,320]{2,1,0:T(8,128)S(1)}, f32[24,32,320]{2,1,0:T(8,128)}) fusion(f32[6,24,32,320]{3,2,1,0:T(8,128)} %param.17), kind=kLoop, calls=%fused_computation.98 | loop fusion | bytes 9830400 | tf_op jit(solution)/shard_map/squeeze | solution.py:73
  24.3 1.0 copy-done.22
  25.6 1.9 collective-permute-start.1
  27.5 0.9 slice_bitcast_fusion.10
  28.4 4.8 %collective-permute-start = (f32[3,32,320]{2,1,0:T(8,128)S(1)}, f32[3,32,320]{2,1,0:T(8,128)S(1)}, u32[]{:S(2)}, u32[]{:S(2)}) collective-permute-start(f32[3,32,320]{2,1,0:T(8,128)S(1)} %pad_maximum_fusion.1), channel_id=1, source_target_pairs={{0,16},{16,32},{32,48},{48,64},{64,80},{80,96},{96,112},{1,17},{17... | collective-permute-start | bytes 368648 | tf_op jit(solution)/shard_map/ppermute | solution.py:14
  33.3 0.6 fusion.79
  33.9 0.6 add_subtract_fusion
  34.5 0.6 iota_subtract_fusion
  35.1 3.9 %slice_bitcast_fusion.7 = (f32[23,32,320]{2,1,0:T(8,128)}, f32[23,32,320]{2,1,0:T(8,128)}, f32[23,32,320]{2,1,0:T(8,128)}) fusion(f32[6,24,32,320]{3,2,1,0:T(8,128)} %param.17), kind=kLoop, calls=%fused_computation.105 | loop fusion | bytes 5652480 | tf_op jit(solution)/shard_map/slice | solution.py:20
  39.0 0.6 add_subtract_fusion.1
  39.8 109.0 %all-reduce.15.cloned.1.call-done = f32[64,96,96]{2,1,0:T(8,128)} async-done(((f32[64,96,96]{2,1,0:T(8,128)}), f32[64,96,96]{2,1,0:T(8,128)}) %all-reduce.15.cloned.1.call-update) | async-done | bytes 2359312 | tf_op jit(solution)/shard_map/psum | solution.py:62
  148.8 1.2 copy-done.13
  150.0 6.0 %fusion.5 = (f32[24,32,320]{2,1,0:T(8,128)S(1)}, f32[24,32,320]{2,1,0:T(8,128)S(1)}) fusion(f32[23,32,320]{2,1,0:T(8,128)} %get-tuple-element.17, f32[1,32,320]{2,1,0:T(8,128)S(1)} %get-tuple-element.46, f32[24,31,320]{2,1,0:T(8,128)} %bitcast.187, f32[24,1,320]{2,1,0:T(1,128)S(1)} %get-tuple-element.43, f32[24,32,319]{2,1,0:T(8,128)} %bitcast.188, ...), kind=kLoop, calls=%fused_computation.9 | loop fusion | flops 4669440 | bytes 15722496 | tf_op jit(solution)/shard_map/add | solution.py:79
  156.0 1.2 slice.421
  157.2 1.5 slice.439
  158.7 1.2 slice.455
  159.9 0.5 copy-done.21
  160.8 3.7 fusion.9
  164.4 1.3 slice.434
  165.7 1.4 slice.454
  167.1 1.1 slice.441
  168.3 0.4 slice.446
  169.0 5.3 %collective-permute-start.3 = (f32[3,24,320]{2,0,1:T(4,128)S(1)}, f32[3,24,320]{2,0,1:T(4,128)S(1)}, u32[]{:S(2)}, u32[]{:S(2)}) collective-permute-start(f32[3,24,320]{2,0,1:T(4,128)S(1)} %pad_maximum_fusion.4), channel_id=1, source_target_pairs={{1,0},{2,1},{3,2},{4,3},{5,4},{6,5},{7,6},{8,7},{9,8},{10,9},{11,1... | collective-permute-start | bytes 276488 | tf_op jit(solution)/shard_map/ppermute | solution.py:14
  174.3 3.1 collective-permute-start.2
  177.4 4.2 %collective-permute-done.3 = f32[3,24,320]{2,0,1:T(4,128)S(1)} collective-permute-done((f32[3,24,320]{2,0,1:T(4,128)S(1)}, f32[3,24,320]{2,0,1:T(4,128)S(1)}, u32[]{:S(2)}, u32[]{:S(2)}) %collective-permute-start.3) | collective-permute-done | bytes 92192 | tf_op jit(solution)/shard_map/ppermute | solution.py:14
  181.7 7.5 %collective-permute-done.2 = f32[3,32,320]{2,1,0:T(8,128)S(1)} collective-permute-done((f32[3,32,320]{2,1,0:T(8,128)S(1)}, f32[3,32,320]{2,1,0:T(8,128)S(1)}, u32[]{:S(2)}, u32[]{:S(2)}) %collective-permute-start.2) | collective-permute-done | bytes 122912 | tf_op jit(solution)/shard_map/ppermute | solution.py:14
  189.2 2.2 fusion.21
  191.5 1.0 copy-done.11
  192.5 1.1 slice.467
  193.6 106.3 %all-reduce.17.cloned.1.call-done = f32[64,96,96]{2,1,0:T(8,128)} async-done(((f32[64,96,96]{2,1,0:T(8,128)}), f32[64,96,96]{2,1,0:T(8,128)}) %all-reduce.17.cloned.1.call-update) | async-done | bytes 2359312 | tf_op jit(solution)/shard_map/psum | solution.py:62
  299.9 4.9 %fusion = f32[24,96,96]{2,0,1:T(8,128)S(1)} fusion(f32[64,96,96]{2,1,0:T(8,128)} %all-reduce.17.cloned.1.call-done, s32[24]{0:T(128)S(1)} %add_subtract_fusion), kind=kOutput, calls=%fused_computation.1 | convolution fusion | flops 169870848 | bytes 3244128 | tf_op jit(solution)/shard_map/Xx,xyz->Xyz/dot_general | solution.py:64
  304.8 0.6 convolution_bitcast_fusion
  305.5 0.6 copy-done.6
  306.1 5.2 %subtract_multiply_fusion = (f32[24,32,320]{2,1,0:T(8,128)}, f32[24,32,320]{2,1,0:T(8,128)S(1)}, f32[24,32,320]{2,1,0:T(8,128)S(1)}, f32[24,32,320]{2,1,0:T(8,128)S(1)}) fusion(f32[24,32,320]{2,1,0:T(8,128)S(1)} %copy-done.2, f32[24,32,320]{2,1,0:T(8,128)S(1)} %copy-done.8, f32[24,32,319]{2,1,0:T(8,128)} %slice.439, f32[6,24,32,320]{3,2,1,0:T(8,128)} %param.17, ...), kind=kOutput, calls=%fused_computation.92 | convolution fusion | flops 289290240 | bytes 17001728 | tf_op jit(solution)/shard_map/xYz,Zz->xYZ/dot_general | solution.py:68
  311.2 0.5 copy-done.24
  311.7 2.2 subtract_multiply_fusion.1
  314.1 0.9 copy-done.16
  314.9 1.1 slice.451
  316.2 1.9 collective-permute-start.5
  318.1 4.2 %collective-permute-start.4 = (f32[3,32,320]{2,1,0:T(8,128)S(1)}, f32[3,32,320]{2,1,0:T(8,128)S(1)}, u32[]{:S(2)}, u32[]{:S(2)}) collective-permute-start(f32[3,32,320]{2,1,0:T(8,128)S(1)} %pad_maximum_fusion.5), channel_id=1, source_target_pairs={{0,16},{16,32},{32,48},{48,64},{64,80},{80,96},{96,112},{1,17},{17... | collective-permute-start | bytes 368648 | tf_op jit(solution)/shard_map/ppermute | solution.py:14
  322.4 2.4 collective-permute-done.5
  324.8 2.9 collective-permute-done.4
  327.7 1.1 fusion.33
  329.0 5.1 %fusion.25 = (f32[24,32,320]{2,1,0:T(8,128)S(1)}, f32[24,32,320]{2,1,0:T(8,128)S(1)}) fusion(f32[24,32,320]{2,1,0:T(8,128)S(1)} %copy-done.6, f32[24,32,320]{2,1,0:T(8,128)} %copy-done.16, f32[23,32,320]{2,1,0:T(8,128)} %slice.451, f32[1,32,320]{2,1,0:T(8,128)S(1)} %get-tuple-element.34, f32[24,32,320]{2,1,0:T(8,128)S(1)} %get-tuple-element.8, ...), kind=kLoop, calls=%fused_computation.40 | loop fusion | flops 4669440 | bytes 15722496 | tf_op jit(solution)/shard_map/add | solution.py:79
  334.3 0.4 slice.481
  334.7 1.1 slice.471
  335.8 1.1 slice.484
  337.0 0.4 slice.486
  337.5 0.4 slice.489
  338.1 4.0 %collective-permute-start.7 = (f32[3,24,320]{2,0,1:T(4,128)S(1)}, f32[3,24,320]{2,0,1:T(4,128)S(1)}, u32[]{:S(2)}, u32[]{:S(2)}) collective-permute-start(f32[3,24,320]{2,0,1:T(4,128)S(1)} %pad_maximum_fusion.8), channel_id=1, source_target_pairs={{1,0},{2,1},{3,2},{4,3},{5,4},{6,5},{7,6},{8,7},{9,8},{10,9},{11,1... | collective-permute-start | bytes 276488 | tf_op jit(solution)/shard_map/ppermute | solution.py:14
  342.2 2.1 pad_maximum_fusion
  344.2 2.4 collective-permute-start.6
  346.7 7.0 %collective-permute-done.6 = f32[3,32,320]{2,1,0:T(8,128)S(1)} collective-permute-done((f32[3,32,320]{2,1,0:T(8,128)S(1)}, f32[3,32,320]{2,1,0:T(8,128)S(1)}, u32[]{:S(2)}, u32[]{:S(2)}) %collective-permute-start.6) | collective-permute-done | bytes 122912 | tf_op jit(solution)/shard_map/ppermute | solution.py:14
  353.7 3.8 %bitcast_dynamic-update-slice_fusion.2 = (f32[6,24,32,320]{3,2,1,0:T(8,128)}, f32[24,32,320]{2,1,0:T(8,128)S(1)}) fusion(f32[24,32,320]{2,1,0:T(8,128)S(1)} %get-tuple-element.52, f32[24,32,320]{2,1,0:T(8,128)S(1)} %copy-done.17, f32[24,32,320]{2,1,0:T(8,128)S(1)} %copy-done.2, f32[24,32,320]{2,1,0:T(8,128)S(1)} %get-tuple-element.23, ...), kind=kLoop, calls=%fused_computation.85 | loop fusion | flops 3932159 | bytes 12973056
  357.6 2.0 bitcast_dynamic-update-slice_fusion.1
  359.5 2.0 bitcast_dynamic-update-slice_fusion
  361.5 2.0 fusion.43
  363.5 2.0 fusion.49
  365.5 2.0 fusion.55
  (107 shorter events, 2.7 us)
Async XLA Ops:
  7.2 1.5 copy-start
  7.2 141.6 %all-reduce.15.cloned.1.call-start = ((), (), s32[]{:S(2)}) async-start(), calls=%async_computation | async-start | bytes 6291456 | tf_op jit(solution)/shard_map/psum | solution.py:62
  8.6 2.5 copy-start.27
  19.5 13.8 %copy-start.28 = (s32[3]{0:T(128)S(1)}, s32[3]{0:T(128)}, u32[]{:S(2)}) copy-start(s32[3]{0:T(128)} %param.15) | copy-start | bytes 40
  19.5 280.4 %all-reduce.17.cloned.1.call-start = ((), (), s32[]{:S(2)}) async-start(), calls=%async_computation.1 | async-start | bytes 6291456 | tf_op jit(solution)/shard_map/psum | solution.py:62
  24.3 1.0 copy-start.22
  24.3 14.7 %copy-start.20 = (f32[24,32,320]{2,1,0:T(8,128)}, f32[24,32,320]{2,1,0:T(8,128)S(1)}, u32[]{:S(2)}) copy-start(f32[24,32,320]{2,1,0:T(8,128)S(1)} %get-tuple-element.14) | copy-start | bytes 2949124
  25.6 14.0 %collective-permute-start.1 = (f32[3,24,320]{2,0,1:T(4,128)S(1)}, f32[3,24,320]{2,0,1:T(4,128)S(1)}, u32[]{:S(2)}, u32[]{:S(2)}) collective-permute-start(f32[3,24,320]{2,0,1:T(4,128)S(1)} %pad_maximum_fusion.2), channel_id=1, source_target_pairs={{0,1},{1,2},{2,3},{3,4},{4,5},{5,6},{6,7},{7,8},{8,9},{9,10},{10,1... | collective-permute-start | bytes 276488 | tf_op jit(solution)/shard_map/ppermute | solution.py:14
  28.4 11.3 %collective-permute-start = (f32[3,32,320]{2,1,0:T(8,128)S(1)}, f32[3,32,320]{2,1,0:T(8,128)S(1)}, u32[]{:S(2)}, u32[]{:S(2)}) collective-permute-start(f32[3,32,320]{2,1,0:T(8,128)S(1)} %pad_maximum_fusion.1), channel_id=1, source_target_pairs={{0,16},{16,32},{32,48},{48,64},{64,80},{80,96},{96,112},{1,17},{17... | collective-permute-start | bytes 368648 | tf_op jit(solution)/shard_map/ppermute | solution.py:14
  148.7 1.3 copy-start.13
  156.0 33.2 %copy-start.5 = (f32[24,32,320]{2,1,0:T(8,128)}, f32[24,32,320]{2,1,0:T(8,128)S(1)}, u32[]{:S(2)}) copy-start(f32[24,32,320]{2,1,0:T(8,128)S(1)} %get-tuple-element.10) | copy-start | bytes 2949124
  156.0 33.2 %copy-start.7 = (f32[24,32,320]{2,1,0:T(8,128)}, f32[24,32,320]{2,1,0:T(8,128)S(1)}, u32[]{:S(2)}) copy-start(f32[24,32,320]{2,1,0:T(8,128)S(1)} %get-tuple-element.11) | copy-start | bytes 2949124
  158.7 1.7 copy-start.21
  158.7 2.0 copy-start.25
  164.4 4.4 %copy-start.9 = (f32[24,32,320]{2,1,0:T(8,128)}, f32[24,32,320]{2,1,0:T(8,128)S(1)}, u32[]{:S(2)}) copy-start(f32[24,32,320]{2,1,0:T(8,128)S(1)} %fusion.9) | copy-start | bytes 2949124
  168.6 20.6 %copy-start.3 = (f32[24,32,320]{2,1,0:T(8,128)S(1)}, f32[24,32,320]{2,1,0:T(8,128)}, u32[]{:S(2)}) copy-start(f32[24,32,320]{2,1,0:T(8,128)} %param.21) | copy-start | bytes 2949124
  168.7 20.5 %copy-start.2 = (f32[24,32,320]{2,1,0:T(8,128)S(1)}, f32[24,32,320]{2,1,0:T(8,128)}, u32[]{:S(2)}) copy-start(f32[24,32,320]{2,1,0:T(8,128)} %param.19) | copy-start | bytes 2949124
  169.0 12.6 %collective-permute-start.3 = (f32[3,24,320]{2,0,1:T(4,128)S(1)}, f32[3,24,320]{2,0,1:T(4,128)S(1)}, u32[]{:S(2)}, u32[]{:S(2)}) collective-permute-start(f32[3,24,320]{2,0,1:T(4,128)S(1)} %pad_maximum_fusion.4), channel_id=1, source_target_pairs={{1,0},{2,1},{3,2},{4,3},{5,4},{6,5},{7,6},{8,7},{9,8},{10,9},{11,1... | collective-permute-start | bytes 276488 | tf_op jit(solution)/shard_map/ppermute | solution.py:14
  174.3 14.9 %collective-permute-start.2 = (f32[3,32,320]{2,1,0:T(8,128)S(1)}, f32[3,32,320]{2,1,0:T(8,128)S(1)}, u32[]{:S(2)}, u32[]{:S(2)}) collective-permute-start(f32[3,32,320]{2,1,0:T(8,128)S(1)} %pad_maximum_fusion.3), channel_id=1, source_target_pairs={{16,0},{32,16},{48,32},{64,48},{80,64},{96,80},{112,96},{17,1},{33... | collective-permute-start | bytes 368648 | tf_op jit(solution)/shard_map/ppermute | solution.py:14
  191.4 1.1 copy-start.11
  299.9 5.6 %copy-start.8 = (f32[24,32,320]{2,1,0:T(8,128)S(1)}, f32[24,32,320]{2,1,0:T(8,128)}, u32[]{:S(2)}) copy-start(f32[24,32,320]{2,1,0:T(8,128)} %copy-done.7) | copy-start | bytes 2949124
  299.9 5.6 %copy-start.10 = (f32[24,32,320]{2,1,0:T(8,128)S(1)}, f32[24,32,320]{2,1,0:T(8,128)}, u32[]{:S(2)}) copy-start(f32[24,32,320]{2,1,0:T(8,128)} %copy-done.9) | copy-start | bytes 2949124
  299.9 5.6 %copy-start.18 = (f32[24,31,320]{2,1,0:T(8,128)S(1)}, f32[24,31,320]{2,1,0:T(8,128)}, u32[]{:S(2)}) copy-start(f32[24,31,320]{2,1,0:T(8,128)} %slice.434) | copy-start | bytes 2856964
  299.9 5.6 %copy-start.19 = (f32[23,32,320]{2,1,0:T(8,128)S(1)}, f32[23,32,320]{2,1,0:T(8,128)}, u32[]{:S(2)}) copy-start(f32[23,32,320]{2,1,0:T(8,128)} %slice.421) | copy-start | bytes 2826244
  304.8 1.3 copy-start.6
  305.4 5.8 %slice-start = ((s8[7077888]{0:T(1024)(128)(4,1)}), s8[4194304]{0:T(1024)(128)(4,1)S(1)}, s32[]{:S(2)}) async-start(s8[7077888]{0:T(1024)(128)(4,1)} %bitcast.175), calls=%async_computation.2 | async-start | bytes 8388608
  306.1 5.2 %slice-start.1 = ((s8[7077888]{0:T(1024)(128)(4,1)}), s8[2883584]{0:T(1024)(128)(4,1)S(1)}, s32[]{:S(2)}) async-start(s8[7077888]{0:T(1024)(128)(4,1)} %bitcast.175), calls=%async_computation.3 | async-start | bytes 5767168
  306.1 5.2 %slice-start.2 = ((f32[24,32,320]{2,1,0:T(8,128)}), f32[23,32,320]{2,1,0:T(8,128)S(1)}, s32[]{:S(2)}) async-start(f32[24,32,320]{2,1,0:T(8,128)} %copy-done.9), calls=%async_computation.4 | async-start | bytes 2260992 | tf_op jit(solution)/shard_map/slice | solution.py:27
  306.1 5.6 %copy-start.24 = (f32[24,31,320]{2,1,0:T(8,128)S(1)}, f32[24,31,320]{2,1,0:T(8,128)}, u32[]{:S(2)}) copy-start(f32[24,31,320]{2,1,0:T(8,128)} %slice.441) | copy-start | bytes 2856964
  313.9 1.0 copy-start.16
  314.9 12.8 %copy-start.14 = (f32[24,32,320]{2,1,0:T(8,128)S(1)}, f32[24,32,320]{2,1,0:T(8,128)}, u32[]{:S(2)}) copy-start(f32[24,32,320]{2,1,0:T(8,128)} %param.20) | copy-start | bytes 2949124
  316.2 8.6 %collective-permute-start.5 = (f32[3,24,320]{2,0,1:T(4,128)S(1)}, f32[3,24,320]{2,0,1:T(4,128)S(1)}, u32[]{:S(2)}, u32[]{:S(2)}) collective-permute-start(f32[3,24,320]{2,0,1:T(4,128)S(1)} %pad_maximum_fusion.6), channel_id=1, source_target_pairs={{0,1},{1,2},{2,3},{3,4},{4,5},{5,6},{6,7},{7,8},{8,9},{9,10},{10,1... | collective-permute-start | bytes 276488 | tf_op jit(solution)/shard_map/ppermute | solution.py:14
  318.1 9.6 %collective-permute-start.4 = (f32[3,32,320]{2,1,0:T(8,128)S(1)}, f32[3,32,320]{2,1,0:T(8,128)S(1)}, u32[]{:S(2)}, u32[]{:S(2)}) collective-permute-start(f32[3,32,320]{2,1,0:T(8,128)S(1)} %pad_maximum_fusion.5), channel_id=1, source_target_pairs={{0,16},{16,32},{32,48},{48,64},{64,80},{80,96},{96,112},{1,17},{17... | collective-permute-start | bytes 368648 | tf_op jit(solution)/shard_map/ppermute | solution.py:14
  327.7 1.3 copy-start.12
  338.1 8.5 %collective-permute-start.7 = (f32[3,24,320]{2,0,1:T(4,128)S(1)}, f32[3,24,320]{2,0,1:T(4,128)S(1)}, u32[]{:S(2)}, u32[]{:S(2)}) collective-permute-start(f32[3,24,320]{2,0,1:T(4,128)S(1)} %pad_maximum_fusion.8), channel_id=1, source_target_pairs={{1,0},{2,1},{3,2},{4,3},{5,4},{6,5},{7,6},{8,7},{9,8},{10,9},{11,1... | collective-permute-start | bytes 276488 | tf_op jit(solution)/shard_map/ppermute | solution.py:14
  342.1 11.6 %copy-start.17 = (f32[24,32,320]{2,1,0:T(8,128)S(1)}, f32[24,32,320]{2,1,0:T(8,128)}, u32[]{:S(2)}) copy-start(f32[24,32,320]{2,1,0:T(8,128)} %copy-done.16) | copy-start | bytes 2949124
  342.1 11.6 %copy-start.23 = (f32[24,32,320]{2,1,0:T(8,128)S(1)}, f32[24,32,320]{2,1,0:T(8,128)}, u32[]{:S(2)}) copy-start(f32[24,32,320]{2,1,0:T(8,128)} %param.18) | copy-start | bytes 2949124
  344.2 9.4 %collective-permute-start.6 = (f32[3,32,320]{2,1,0:T(8,128)S(1)}, f32[3,32,320]{2,1,0:T(8,128)S(1)}, u32[]{:S(2)}, u32[]{:S(2)}) collective-permute-start(f32[3,32,320]{2,1,0:T(8,128)S(1)} %pad_maximum_fusion.7), channel_id=1, source_target_pairs={{16,0},{32,16},{48,32},{64,48},{80,64},{96,80},{112,96},{17,1},{33... | collective-permute-start | bytes 368648 | tf_op jit(solution)/shard_map/ppermute | solution.py:14
  357.6 2.0 copy-start.15
  359.5 2.0 copy-start.26
  363.5 2.0 copy-start.4
  365.5 2.0 copy-start.1
Sparse Core Ops, SparseCore 0:
  19.6 129.0 all-reduce.14
  151.3 148.6 all-reduce.16
